TPU v7x, 256 devices: a whole 4x4x8 slice. The times are simulated.
256 devices in a mesh: rep: 64 (over z, x, core), tp: 4 (over y).
Axes of the slice: x: 4, y: 4, z: 8, core: 2. Of those that a mesh axis runs over, the one named last changes fastest.
Arguments:
- suffix_source: bfloat16 [64, 384, 4096], P('rep', None, 'tp'), may hold values from -6 to 6
- suffix_accept: bfloat16 [64, 384, 4096], P('rep', None, 'tp'), may hold values from -3 to 3
- suffix_address: bfloat16 [64, 384, 4096], P('rep', None, 'tp'), may hold values from -3 to 3
- guess_lane_source: bfloat16 [128, 16, 4096], P('rep', None, 'tp'), may hold values from -6 to 6
- guess_lane_accept: bfloat16 [128, 16, 4096], P('rep', None, 'tp'), may hold values from -3 to 3
- guess_lane_address: bfloat16 [128, 16, 4096], P('rep', None, 'tp'), may hold values from -3 to 3
- content_map: bfloat16 [4096, 4096], P(None, 'tp'), may hold values from -0.09375 to 0.09375
- forget_shrink_map: bfloat16 [4096, 128], replicated, may hold values from -0.09375 to 0.09375
- forget_expand_map: bfloat16 [128, 4096], P(None, 'tp'), may hold values from -0.35351562 to 0.35351562
- forget_lane_anchor: float32 [4096], P('tp'), may hold values from -12 to -3
- present_boost: float32 [4096], P('tp'), may hold values from -1.5 to 1.5
- content_blend_share: float32 [4096], P('tp'), may hold values from 0 to 1
- forget_blend_share: float32 [4096], P('tp'), may hold values from 0 to 1
- lane_normal_scale: float32 [4096], P('tp'), may hold values from 0.5 to 1.5
- lane_normal_shift: float32 [4096], P('tp'), may hold values from -1.2 to 1.2
- kernel_memory_saved: float32 [128, 64, 4096], P(None, 'rep', 'tp'), may hold values from -6 to 6
- prior_source_saved: bfloat16 [128, 64, 64], P(None, 'rep', 'tp'), may hold values from -6 to 6
- lane_owner: int32 [128], replicated, may hold values from 0 to 127, as said below
- request_spans: int32 [128], replicated, may hold values from 16 to 400, as said below
- admitted_guesses: int32 [128], replicated, may hold values from 0 to 16
Outputs:
- tail_out: bfloat16 [64, 384, 4096], P('rep', None, 'tp')
- draft_out: bfloat16 [128, 16, 4096], P('rep', None, 'tp')
- state_out: float32 [128, 64, 4096], P(None, 'rep', 'tp')
- shift_out: bfloat16 [128, 64, 64], P(None, 'rep', 'tp')
Inputs may be any that keep to these rules, and one draw needn't show every extreme that they name: `lane_owner`: a permutation of the request numbers. `request_spans`: exactly 8 requests have 16 + 384 tokens and the others 16; a long request is always dealt to a slot s with s % 2 == 0; each aligned block of 8 consecutive groups holds exactly one group whose first slot is long; the tail buffers of groups whose first slot is not long are not read.
All inputs are finite; a program needn't handle non-finite values.
Results may differ from a plain program's by a relative error of at most 0.0051.
The roundings to bfloat16 on the way count: a program that leaves them out, or rounds other values in their place, can miss the bound.
Values may be sent and summed in bfloat16 or wider, within the bound.
A program may use at most 128 MiB of HBM per device.

v0:
```python
import jax
import jax.numpy as jnp
from jax import lax
from jax.sharding import PartitionSpec as P

SUBSPACE_SPAN = 64
DRAFT = 16
HIGH = lax.Precision.HIGHEST
EPS = 0.00064


def group_norm(answer_collection, lane_normal_scale, lane_normal_shift):
    center = answer_collection - jnp.mean(answer_collection, axis=-1, keepdims=True)
    spread = jnp.mean(center * center, axis=-1, keepdims=True)
    normed = (center / jnp.sqrt(spread + EPS)).reshape(answer_collection.shape[0], -1)
    return (normed * lane_normal_scale + lane_normal_shift).astype(jnp.bfloat16)


def token_mix(current, previous, mixing):
    present = current.astype(jnp.float32)
    return (present + (previous.astype(jnp.float32) - present) * mixing).astype(jnp.bfloat16)


def project(
    mixed_value,
    decay_mixed_input,
    content_map,
    forget_shrink_map,
    forget_expand_map,
    forget_lane_anchor,
):
    acc_value = jnp.dot(
        lax.all_gather(mixed_value, "tp", axis=1, tiled=True),
        content_map,
        preferred_element_type=jnp.float32,
    )
    decay_accumulated = jnp.dot(
        lax.all_gather(decay_mixed_input, "tp", axis=1, tiled=True),
        forget_shrink_map,
        preferred_element_type=jnp.float32,
    )
    acc_value, decay_accumulated = (acc_value, decay_accumulated)
    content_vectors = acc_value.astype(jnp.bfloat16)
    decay_low_rank = jnp.tanh(decay_accumulated).astype(jnp.bfloat16)
    forget_logscale = -jnp.exp(
        forget_lane_anchor
        + jnp.dot(decay_low_rank, forget_expand_map, preferred_element_type=jnp.float32)
    )
    return (content_vectors, forget_logscale)


def process_blocks(
    accept_vectors, address_vectors, content_vectors, forget_logscale, ongoing_memory, lanes_boost
):
    total_steps = accept_vectors.shape[0]
    block_len = min(64, total_steps)
    block_count = total_steps // block_len
    lower = jnp.arange(block_len)[:, None] > jnp.arange(block_len)[None, :]

    def shape_blocks(array):
        return array.reshape(block_count, block_len, array.shape[1], array.shape[2])

    def one_block(threaded_pair, source_vectors):
        accept_vectors_all, address_vectors_all, value_rows_batch, rate_b = source_vectors
        inclusive = jnp.cumsum(rate_b, axis=0)
        exclusive = inclusive - rate_b
        middle = inclusive[block_len // 2]
        recept_scaled = accept_vectors_all * jnp.exp(exclusive - middle)
        keys_scaled = address_vectors_all * jnp.exp(middle - inclusive)
        scores = jnp.einsum("thi,shi->hts", recept_scaled, keys_scaled, precision=HIGH)
        scores = jnp.where(lower[None], scores, 0.0)
        answer_vectors = jnp.einsum("hts,shj->thj", scores, value_rows_batch, precision=HIGH)
        answer_vectors = answer_vectors + jnp.einsum(
            "thi,hij->thj", accept_vectors_all * jnp.exp(exclusive), threaded_pair, precision=HIGH
        )
        answer_vectors = (
            answer_vectors
            + jnp.sum(
                accept_vectors_all * lanes_boost * address_vectors_all, axis=-1, keepdims=True
            )
            * value_rows_batch
        )
        total = inclusive[-1]
        threaded_pair = jnp.exp(total)[:, :, None] * threaded_pair + jnp.einsum(
            "shi,shj->hij",
            address_vectors_all * jnp.exp(total - inclusive),
            value_rows_batch,
            precision=HIGH,
        )
        return (threaded_pair, answer_vectors)

    closing_answer, answer_collection = lax.scan(
        one_block,
        ongoing_memory,
        (
            shape_blocks(accept_vectors),
            shape_blocks(address_vectors),
            shape_blocks(content_vectors),
            shape_blocks(forget_logscale),
        ),
    )
    return (
        answer_collection.reshape(total_steps, accept_vectors.shape[1], accept_vectors.shape[2]),
        closing_answer,
    )


def local(
    suffix_source,
    suffix_accept,
    suffix_address,
    guess_lane_source,
    guess_lane_accept,
    guess_lane_address,
    content_map,
    forget_shrink_map,
    forget_expand_map,
    forget_lane_anchor,
    present_boost,
    content_blend_share,
    forget_blend_share,
    lane_normal_scale,
    lane_normal_shift,
    kernel_memory_saved,
    prior_source_saved,
    lane_owner,
    request_spans,
    admitted_guesses,
):
    local_width = content_map.shape[1]
    lanes_owned = local_width // SUBSPACE_SPAN
    slots = guess_lane_source.shape[0]
    squad_index = lax.axis_index("rep")
    slot_ids = squad_index * slots + jnp.arange(slots, dtype=jnp.int32)
    my_reqs = lane_owner[slot_ids]
    slot_long = request_spans[my_reqs] > DRAFT
    group_long = slot_long[0]
    lanes_boost = present_boost.reshape(lanes_owned, SUBSPACE_SPAN)
    ordered_state = kernel_memory_saved[lane_owner]
    ordered_shift = prior_source_saved[lane_owner].astype(jnp.float32)
    got_state, got_shift = (
        lax.all_to_all(ordered_state, "rep", split_axis=0, concat_axis=1, tiled=True),
        lax.all_to_all(ordered_shift, "rep", split_axis=0, concat_axis=1, tiled=True),
    )
    start = got_state.reshape(slots, SUBSPACE_SPAN, lanes_owned, SUBSPACE_SPAN).transpose(
        0, 2, 1, 3
    )
    start_prev = got_shift.astype(jnp.bfloat16).transpose(0, 2, 1).reshape(slots, local_width)

    def divide_lanes(array):
        return array.astype(jnp.float32).reshape(array.shape[0], lanes_owned, SUBSPACE_SPAN)

    tail_tokens = suffix_source[0]
    tail_len = tail_tokens.shape[0]
    tail_prev = jnp.concatenate([start_prev[:1], tail_tokens[:-1]], axis=0)
    tail_value = token_mix(tail_tokens, tail_prev, content_blend_share)
    tail_decay = token_mix(tail_tokens, tail_prev, forget_blend_share)
    tail_recept = suffix_accept[0]
    tail_keys = suffix_address[0]
    first = jnp.where(slot_long[:, None], tail_tokens[-1][None, :], start_prev)
    draft_prev = jnp.concatenate([first[:, None], guess_lane_source[:, :-1]], axis=1)
    draft_value = token_mix(guess_lane_source, draft_prev, content_blend_share).reshape(
        slots * DRAFT, local_width
    )
    draft_decay = token_mix(guess_lane_source, draft_prev, forget_blend_share).reshape(
        slots * DRAFT, local_width
    )
    content_vectors, forget_logscale = project(
        jnp.concatenate([tail_value, draft_value], axis=0),
        jnp.concatenate([tail_decay, draft_decay], axis=0),
        content_map,
        forget_shrink_map,
        forget_expand_map,
        forget_lane_anchor,
    )
    tail_y, tail_end = process_blocks(
        divide_lanes(tail_recept),
        divide_lanes(tail_keys),
        divide_lanes(content_vectors[:tail_len]),
        forget_logscale[:tail_len].reshape(tail_len, lanes_owned, SUBSPACE_SPAN),
        start[0],
        lanes_boost,
    )
    tail_norm = group_norm(tail_y, lane_normal_scale, lane_normal_shift)
    tail_out = jnp.where(group_long, tail_norm, jnp.zeros_like(tail_norm))[None]
    guess_content = (
        content_vectors[tail_len:]
        .astype(jnp.float32)
        .reshape(slots, DRAFT, lanes_owned, SUBSPACE_SPAN)
    )
    guess_forget = forget_logscale[tail_len:].reshape(slots, DRAFT, lanes_owned, SUBSPACE_SPAN)
    guess_accept = guess_lane_accept.astype(jnp.float32).reshape(
        slots, DRAFT, lanes_owned, SUBSPACE_SPAN
    )
    guess_address = guess_lane_address.astype(jnp.float32).reshape(
        slots, DRAFT, lanes_owned, SUBSPACE_SPAN
    )
    trailing_pair = jnp.where(slot_long[:, None, None, None], tail_end[None], start)
    draft_y, draft_final = jax.vmap(process_blocks, in_axes=(0, 0, 0, 0, 0, None))(
        guess_accept, guess_address, guess_content, guess_forget, trailing_pair, lanes_boost
    )
    draft_out = group_norm(
        draft_y.reshape(slots * DRAFT, lanes_owned, SUBSPACE_SPAN),
        lane_normal_scale,
        lane_normal_shift,
    ).reshape(slots, DRAFT, local_width)
    count = admitted_guesses[my_reqs]
    taken = jnp.arange(DRAFT, dtype=jnp.int32)[None, :] < count[:, None]
    inclusive_d = jnp.cumsum(guess_forget, axis=1)
    upto = jnp.sum(jnp.where(taken[:, :, None, None], guess_forget, 0.0), axis=1)
    weight = jnp.where(taken[:, :, None, None], jnp.exp(upto[:, None] - inclusive_d), 0.0)
    chosen = jnp.exp(upto)[..., None] * trailing_pair + jnp.einsum(
        "sthi,sthj->shij", guess_address * weight, guess_content, precision=HIGH
    )
    edge_row = guess_lane_source[jnp.arange(slots), jnp.maximum(count - 1, 0)]
    edge = jnp.where((count > 0)[:, None], edge_row, first)
    ret_state = chosen.transpose(0, 2, 1, 3).reshape(slots, SUBSPACE_SPAN, local_width)
    ret_shift = (
        edge.reshape(slots, lanes_owned, SUBSPACE_SPAN).transpose(0, 2, 1).astype(jnp.float32)
    )
    back_state, back_shift = (
        lax.all_to_all(ret_state, "rep", split_axis=1, concat_axis=0, tiled=True),
        lax.all_to_all(ret_shift, "rep", split_axis=1, concat_axis=0, tiled=True),
    )
    total_reqs = lane_owner.shape[0]
    inverse = (
        jnp.zeros((total_reqs,), jnp.int32)
        .at[lane_owner]
        .set(jnp.arange(total_reqs, dtype=jnp.int32))
    )
    state_out = back_state[inverse]
    shift_out = back_shift[inverse].astype(jnp.bfloat16)
    return (tail_out, draft_out, state_out, shift_out)


def solution(mesh):
    placed = (
        P("rep", None, "tp"),
        P("rep", None, "tp"),
        P("rep", None, "tp"),
        P("rep", None, "tp"),
        P("rep", None, "tp"),
        P("rep", None, "tp"),
        P(None, "tp"),
        P(),
        P(None, "tp"),
        P("tp"),
        P("tp"),
        P("tp"),
        P("tp"),
        P("tp"),
        P("tp"),
        P(None, "rep", "tp"),
        P(None, "rep", "tp"),
        P(),
        P(),
        P(),
    )
    return jax.shard_map(
        local,
        mesh=mesh,
        in_specs=placed,
        out_specs=(
            P("rep", None, "tp"),
            P("rep", None, "tp"),
            P(None, "rep", "tp"),
            P(None, "rep", "tp"),
        ),
        check_vma=False,
    )
```

profile of v0, /device:TPU:1, one launch (start us, length us, event | category | flops | bytes accessed | tf_op | source)
XLA Modules:
  0.0 245.0 jit_solution(6929239159110475393)
XLA Ops:
  10.2 13.0 %all-to-all-start.1 = ((bf16[128,1,16]{2,1,0:T(2,128)(2,1)}), bf16[128,1,16]{2,1,0:T(2,128)(2,1)S(1)}, u32[]{:S(2)}, u32[]{:S(2)}) async-start(bf16[128,1,16]{2,1,0:T(2,128)(2,1)} %convert.36), calls=%async_computation.1 | async-start | bytes 131072 | tf_op jit(solution)/shard_map/all_to_all | solution.py:143
  23.3 1.3 gather_fusion
  24.6 1.3 gather_fusion.1
  26.0 7.3 %all-to-all-done.1 = bf16[128,1,16]{2,1,0:T(2,128)(2,1)S(1)} async-done(((bf16[128,1,16]{2,1,0:T(2,128)(2,1)}), bf16[128,1,16]{2,1,0:T(2,128)(2,1)S(1)}, u32[]{:S(2)}, u32[]{:S(2)}) %all-to-all-start.1) | async-done | bytes 4128 | tf_op jit(solution)/shard_map/all_to_all | solution.py:143
  39.5 4.4 %all-to-all-start.3 = ((bf16[2,64,16]{2,0,1:T(2,128)(2,1)}), bf16[2,64,16]{2,0,1:T(2,128)(2,1)S(1)}, u32[]{:S(2)}, u32[]{:S(2)}) async-start(bf16[2,64,16]{2,0,1:T(2,128)(2,1)} %convert_bitcast_fusion), calls=%async_computation.3 | async-start | bytes 65536 | tf_op jit(solution)/shard_map/all_to_all | solution.py:223
  44.9 1.3 copy.156
  46.2 7.1 %all-to-all-done.3 = bf16[2,64,16]{2,0,1:T(2,128)(2,1)S(1)} async-done(((bf16[2,64,16]{2,0,1:T(2,128)(2,1)}), bf16[2,64,16]{2,0,1:T(2,128)(2,1)S(1)}, u32[]{:S(2)}, u32[]{:S(2)}) %all-to-all-start.3) | async-done | bytes 4128 | tf_op jit(solution)/shard_map/all_to_all | solution.py:223
  53.3 4.7 %all-to-all-start = ((f32[128,1,1024]{2,1,0:T(1,128)}), f32[128,1,1024]{2,1,0:T(1,128)S(1)}, u32[]{:S(2)}, u32[]{:S(2)}) async-start(f32[128,1,1024]{2,1,0:T(1,128)} %copy.156), calls=%async_computation | async-start | bytes 1048576 | tf_op jit(solution)/shard_map/all_to_all | solution.py:142
  58.1 1.2 scatter_custom_fusion
  61.0 2.2 reshape.402
  63.2 3.4 %reshape.400 = f32[6,64,16,64]{3,2,1,0:T(8,128)} reshape(bf16[1,384,1024]{2,1,0:T(8,128)(2,1)} %param.24) | data formatting | bytes 2359296 | tf_op jit(solution)/shard_map/convert_element_type | solution.py:151
  69.2 6.7 %all-to-all-done = f32[128,1,1024]{2,1,0:T(1,128)S(1)} async-done(((f32[128,1,1024]{2,1,0:T(1,128)}), f32[128,1,1024]{2,1,0:T(1,128)S(1)}, u32[]{:S(2)}, u32[]{:S(2)}) %all-to-all-start) | async-done | bytes 524320 | tf_op jit(solution)/shard_map/all_to_all | solution.py:142
  77.6 8.1 %convolution_convert_fusion = bf16[416,1024]{1,0:T(8,128)(2,1)S(1)} fusion(bf16[416,4096]{1,0:T(8,128)(2,1)} %all-gather.5.cloned.1.call-done, bf16[4096,1024]{1,0:T(8,128)(2,1)} %param.28), kind=kOutput, calls=%fused_computation.48 | convolution fusion | flops 3490086912 | bytes 12648448 | tf_op jit(solution)/shard_map/dot_general | solution.py:32
  86.3 1.4 slice_convert_fusion
  87.7 33.6 %all-gather.3.cloned.1.call-done = bf16[416,4096]{1,0:T(8,128)(2,1)} async-done(((bf16[416,1024]{1,0:T(8,128)(2,1)}), bf16[416,4096]{1,0:T(8,128)(2,1)}) %all-gather.3.cloned.1.call-update) | async-done | bytes 3407888 | tf_op jit(solution)/shard_map/all_gather | solution.py:38
  121.3 3.7 %exponential_negate_fusion = f32[416,1024]{1,0:T(8,128)S(1)} fusion(bf16[128,1024]{1,0:T(8,128)(2,1)S(1)} %copy-done.18, bf16[416,4096]{1,0:T(8,128)(2,1)} %all-gather.3.cloned.1.call-done, bf16[4096,128]{1,0:T(8,128)(2,1)S(1)} %copy-done, f32[1024]{0:T(1024)} %param.31), kind=kOutput, calls=%fused_computation.44 | convolution fusion | flops 546164736 | bytes 6426624 | tf_op jit(solution)/shard_map/dot_general | solution.py:47
  125.1 1.1 copy-done.7
  126.4 1.4 fusion.41
  128.0 1.1 select_multiply_fusion
  129.2 2.2 reshape_reshape.7
  131.4 3.4 %reshape.401 = f32[6,64,16,64]{3,2,1,0:T(8,128)} reshape(f32[384,1024]{1,0:T(8,128)} %slice_convert_fusion) | data formatting | bytes 3145728 | tf_op jit(solution)/shard_map/reshape;reshape | solution.py:61
  134.8 60.3 %while.3 = (s32[]{:T(128)}, f32[16,64,64]{2,1,0:T(8,128)S(1)}, f32[6,64,16,64]{3,1,2,0:T(8,128)}, f32[6,64,16,64]{3,2,1,0:T(8,128)}, f32[6,64,16,64]{3,2,1,0:T(8...) while((s32[]{:T(128)}, f32[16,64,64]{2,1,0:T(8,128)S(1)}, ...), condition=%wide.region_3.4_spmd.clone, body=%wide.region_0.3_spmd.clone.sunk | while | flops 206572544 | bytes 8724625 | solution.py:92
  135.9 1.1 fusion.68
  137.1 2.5 %bitcast_multiply_fusion.6 = (f32[64,16,64]{2,1,0:T(8,128)S(1)}, f32[64,16,64]{2,1,0:T(8,128)S(1)}, f32[64,16]{1,0:T(8,128)S(1)}, f32[64,16,64]{2,1,0:T(8,128)S(1)}, f32[64,16,64]{2,1,0:T(8,128)}) fusion(f32[64,16,64]{2,1,0:T(8,128)S(1)} %fusion.68, f32[6,64,16,64]{3,2,1,0:T(8,128)} %get-tuple-element.282, s32[]{:T(128)S(6)} %copy.261, ...), kind=kLoop, calls=%fused_computation.24.clone.1 | loop fusion | flops 719872 | bytes 2113540 | tf_op jit(solution)/shard_map/while/body/eval_jaxpr/mul | solution.py:69
  139.7 1.3 convolution_select_fusion.3
  141.7 1.8 fusion.70
  143.5 1.3 convolution_add_fusion.3
  146.0 1.1 fusion.68
  147.1 2.5 %bitcast_multiply_fusion.6 = (f32[64,16,64]{2,1,0:T(8,128)S(1)}, f32[64,16,64]{2,1,0:T(8,128)S(1)}, f32[64,16]{1,0:T(8,128)S(1)}, f32[64,16,64]{2,1,0:T(8,128)S(1)}, f32[64,16,64]{2,1,0:T(8,128)}) fusion(f32[64,16,64]{2,1,0:T(8,128)S(1)} %fusion.68, f32[6,64,16,64]{3,2,1,0:T(8,128)} %get-tuple-element.282, s32[]{:T(128)S(6)} %copy.261, ...), kind=kLoop, calls=%fused_computation.24.clone.1 | loop fusion | flops 719872 | bytes 2113540 | tf_op jit(solution)/shard_map/while/body/eval_jaxpr/mul | solution.py:69
  149.7 1.3 convolution_select_fusion.3
  151.8 1.8 fusion.70
  153.6 1.3 convolution_add_fusion.3
  156.1 1.1 fusion.68
  157.2 2.5 %bitcast_multiply_fusion.6 = (f32[64,16,64]{2,1,0:T(8,128)S(1)}, f32[64,16,64]{2,1,0:T(8,128)S(1)}, f32[64,16]{1,0:T(8,128)S(1)}, f32[64,16,64]{2,1,0:T(8,128)S(1)}, f32[64,16,64]{2,1,0:T(8,128)}) fusion(f32[64,16,64]{2,1,0:T(8,128)S(1)} %fusion.68, f32[6,64,16,64]{3,2,1,0:T(8,128)} %get-tuple-element.282, s32[]{:T(128)S(6)} %copy.261, ...), kind=kLoop, calls=%fused_computation.24.clone.1 | loop fusion | flops 719872 | bytes 2113540 | tf_op jit(solution)/shard_map/while/body/eval_jaxpr/mul | solution.py:69
  159.8 1.3 convolution_select_fusion.3
  161.8 1.8 fusion.70
  163.6 1.3 convolution_add_fusion.3
  166.1 1.1 fusion.68
  167.2 2.5 %bitcast_multiply_fusion.6 = (f32[64,16,64]{2,1,0:T(8,128)S(1)}, f32[64,16,64]{2,1,0:T(8,128)S(1)}, f32[64,16]{1,0:T(8,128)S(1)}, f32[64,16,64]{2,1,0:T(8,128)S(1)}, f32[64,16,64]{2,1,0:T(8,128)}) fusion(f32[64,16,64]{2,1,0:T(8,128)S(1)} %fusion.68, f32[6,64,16,64]{3,2,1,0:T(8,128)} %get-tuple-element.282, s32[]{:T(128)S(6)} %copy.261, ...), kind=kLoop, calls=%fused_computation.24.clone.1 | loop fusion | flops 719872 | bytes 2113540 | tf_op jit(solution)/shard_map/while/body/eval_jaxpr/mul | solution.py:69
  169.8 1.3 convolution_select_fusion.3
  171.9 1.8 fusion.70
  173.7 1.3 convolution_add_fusion.3
  176.2 1.1 fusion.68
  177.3 2.5 %bitcast_multiply_fusion.6 = (f32[64,16,64]{2,1,0:T(8,128)S(1)}, f32[64,16,64]{2,1,0:T(8,128)S(1)}, f32[64,16]{1,0:T(8,128)S(1)}, f32[64,16,64]{2,1,0:T(8,128)S(1)}, f32[64,16,64]{2,1,0:T(8,128)}) fusion(f32[64,16,64]{2,1,0:T(8,128)S(1)} %fusion.68, f32[6,64,16,64]{3,2,1,0:T(8,128)} %get-tuple-element.282, s32[]{:T(128)S(6)} %copy.261, ...), kind=kLoop, calls=%fused_computation.24.clone.1 | loop fusion | flops 719872 | bytes 2113540 | tf_op jit(solution)/shard_map/while/body/eval_jaxpr/mul | solution.py:69
  179.9 1.3 convolution_select_fusion.3
  182.0 1.8 fusion.70
  183.7 1.3 convolution_add_fusion.3
  186.2 1.1 fusion.68
  187.3 2.5 %bitcast_multiply_fusion.6 = (f32[64,16,64]{2,1,0:T(8,128)S(1)}, f32[64,16,64]{2,1,0:T(8,128)S(1)}, f32[64,16]{1,0:T(8,128)S(1)}, f32[64,16,64]{2,1,0:T(8,128)S(1)}, f32[64,16,64]{2,1,0:T(8,128)}) fusion(f32[64,16,64]{2,1,0:T(8,128)S(1)} %fusion.68, f32[6,64,16,64]{3,2,1,0:T(8,128)} %get-tuple-element.282, s32[]{:T(128)S(6)} %copy.261, ...), kind=kLoop, calls=%fused_computation.24.clone.1 | loop fusion | flops 719872 | bytes 2113540 | tf_op jit(solution)/shard_map/while/body/eval_jaxpr/mul | solution.py:69
  189.9 1.3 convolution_select_fusion.3
  192.0 1.8 fusion.70
  193.8 1.3 convolution_add_fusion.3
  195.1 2.8 %reduce_sum.64 = f32[6,64,16]{1,2,0:T(8,128)S(1)} reduce(f32[6,64,16,64]{3,1,2,0:T(8,128)} %get-tuple-element.79, f32[]{:T(128)} %constant.69.clone.1), dimensions={3}, to_apply=%region_4.5 | reduce | flops 387072 | bytes 1597444 | tf_op jit(solution)/shard_map/reduce_sum | solution.py:13
  197.9 3.3 %multiply_reduce_fusion = f32[6,64,16]{1,2,0:T(8,128)S(1)} fusion(f32[6,64,16,64]{3,1,2,0:T(8,128)} %get-tuple-element.79, f32[6,64,16]{1,2,0:T(8,128)S(1)} %broadcast_multiply_fusion), kind=kLoop, calls=%fused_computation.40 | loop fusion | flops 1173504 | bytes 1622016 | tf_op jit(solution)/shard_map/reduce_sum | solution.py:14
  202.2 1.4 fusion.19
  204.2 1.3 reshape.497
  205.5 10.8 %all-to-all-start.2 = ((f32[2,64,1024]{2,0,1:T(2,128)}), f32[2,64,1024]{2,0,1:T(2,128)S(1)}, u32[]{:S(2)}, u32[]{:S(2)}) async-start(f32[2,64,1024]{2,0,1:T(2,128)} %reshape.497), calls=%async_computation.2 | async-start | bytes 1048576 | tf_op jit(solution)/shard_map/all_to_all | solution.py:222
  216.4 1.3 fusion.24
  218.9 3.5 %copy.165 = f32[6,64,16,64]{3,2,1,0:T(8,128)} copy(f32[6,64,16,64]{3,1,2,0:T(8,128)S(1)} %copy-done.4) | data formatting | bytes 3145728 | tf_op jit(solution)/shard_map/while | solution.py:92
  222.3 3.7 %reshape.397 = f32[1,384,1024]{2,1,0:T(8,128)} reshape(f32[6,64,16,64]{3,2,1,0:T(8,128)} %copy.165) | data formatting | bytes 3145728 | tf_op jit(solution)/shard_map/reshape | solution.py:103
  227.5 1.6 copy.167
  229.2 1.6 copy.169
  231.5 3.9 %fusion.26 = bf16[1,384,1024]{2,1,0:T(8,128)(2,1)} fusion(f32[1024]{0:T(1024)S(1)} %copy-done.26, f32[1024]{0:T(1024)S(1)} %copy-done.27, f32[1,384,1024]{2,1,0:T(8,128)} %copy.169, f32[1,384,1024]{2,1,0:T(8,128)} %reshape.397, f32[1,384,1024]{2,1,0:T(8,128)} %copy.167, pred[]{:T(512)S(1)} %bitcast.201), kind=kLoop, calls=%fused_computation.66 | loop fusion | flops 2359296 | bytes 5513217 | tf_op jit(solution)/shard_map/jit(_where)/select_n | solution.py:185
  236.8 1.3 copy.190
  (206 shorter events, 35.7 us)
Async XLA Ops:
  7.2 114.1 %copy-start = (bf16[4096,128]{1,0:T(8,128)(2,1)S(1)}, bf16[4096,128]{1,0:T(8,128)(2,1)}, u32[]{:S(2)}) copy-start(bf16[4096,128]{1,0:T(8,128)(2,1)} %param.29) | copy-start | bytes 3145732
  7.2 18.7 %copy-start.8 = (bf16[1,384,1024]{2,1,0:T(8,128)(2,1)S(1)}, bf16[1,384,1024]{2,1,0:T(8,128)(2,1)}, u32[]{:S(2)}) copy-start(bf16[1,384,1024]{2,1,0:T(8,128)(2,1)} %param.22) | copy-start | bytes 2359300
  8.8 25.0 %copy-start.17 = (bf16[2,16,1024]{2,1,0:T(8,128)(2,1)S(1)}, bf16[2,16,1024]{2,1,0:T(8,128)(2,1)}, u32[]{:S(2)}) copy-start(bf16[2,16,1024]{2,1,0:T(8,128)(2,1)} %param.25) | copy-start | bytes 196612
  8.8 25.0 %copy-start.24 = (f32[1024]{0:T(1024)S(1)}, f32[1024]{0:T(1024)}, u32[]{:S(2)}) copy-start(f32[1024]{0:T(1024)} %param.33) | copy-start | bytes 12292
  8.8 25.0 %copy-start.25 = (f32[1024]{0:T(1024)S(1)}, f32[1024]{0:T(1024)}, u32[]{:S(2)}) copy-start(f32[1024]{0:T(1024)} %param.34) | copy-start | bytes 12292
  10.2 23.1 %all-to-all-start.1 = ((bf16[128,1,16]{2,1,0:T(2,128)(2,1)}), bf16[128,1,16]{2,1,0:T(2,128)(2,1)S(1)}, u32[]{:S(2)}, u32[]{:S(2)}) async-start(bf16[128,1,16]{2,1,0:T(2,128)(2,1)} %convert.36), calls=%async_computation.1 | async-start | bytes 131072 | tf_op jit(solution)/shard_map/all_to_all | solution.py:143
  23.2 54.4 %all-gather.5.cloned.1.call-start = ((), (), s32[]{:S(2)}) async-start(), calls=%async_computation.5 | async-start | bytes 4259840 | tf_op jit(solution)/shard_map/all_gather | solution.py:33
  35.0 1.1 copy-start.20
  36.0 1.2 copy-start.2
  36.0 7.9 %copy-start.16 = (f32[128,1,1024]{2,1,0:T(1,128)S(1)}, f32[128,1,1024]{2,1,0:T(1,128)}, u32[]{:S(2)}) copy-start(f32[128,1,1024]{2,1,0:T(1,128)} %param.37) | copy-start | bytes 1572868
  36.0 85.2 %all-gather.3.cloned.1.call-start = ((), (), s32[]{:S(2)}) async-start(), calls=%async_computation.4 | async-start | bytes 4259840 | tf_op jit(solution)/shard_map/all_gather | solution.py:38
  39.5 13.8 %all-to-all-start.3 = ((bf16[2,64,16]{2,0,1:T(2,128)(2,1)}), bf16[2,64,16]{2,0,1:T(2,128)(2,1)S(1)}, u32[]{:S(2)}, u32[]{:S(2)}) async-start(bf16[2,64,16]{2,0,1:T(2,128)(2,1)} %convert_bitcast_fusion), calls=%async_computation.3 | async-start | bytes 65536 | tf_op jit(solution)/shard_map/all_to_all | solution.py:223
  44.8 14.4 %copy-start.21 = (f32[1024]{0:T(1024)S(1)}, f32[1024]{0:T(1024)}, u32[]{:S(2)}) copy-start(f32[1024]{0:T(1024)} %param.32) | copy-start | bytes 12292
  44.8 14.5 %copy-start.22 = (bf16[2,16,1024]{2,1,0:T(8,128)(2,1)S(1)}, bf16[2,16,1024]{2,1,0:T(8,128)(2,1)}, u32[]{:S(2)}) copy-start(bf16[2,16,1024]{2,1,0:T(8,128)(2,1)} %param.26) | copy-start | bytes 196612
  44.8 15.3 %copy-start.23 = (bf16[2,16,1024]{2,1,0:T(8,128)(2,1)S(1)}, bf16[2,16,1024]{2,1,0:T(8,128)(2,1)}, u32[]{:S(2)}) copy-start(bf16[2,16,1024]{2,1,0:T(8,128)(2,1)} %param.27) | copy-start | bytes 196612
  44.9 16.2 %copy-start.15 = (bf16[1,384,1024]{2,1,0:T(8,128)(2,1)S(1)}, bf16[1,384,1024]{2,1,0:T(8,128)(2,1)}, u32[]{:S(2)}) copy-start(bf16[1,384,1024]{2,1,0:T(8,128)(2,1)} %param.23) | copy-start | bytes 2359300
  53.3 22.6 %all-to-all-start = ((f32[128,1,1024]{2,1,0:T(1,128)}), f32[128,1,1024]{2,1,0:T(1,128)S(1)}, u32[]{:S(2)}, u32[]{:S(2)}) async-start(f32[128,1,1024]{2,1,0:T(1,128)} %copy.156), calls=%async_computation | async-start | bytes 1048576 | tf_op jit(solution)/shard_map/all_to_all | solution.py:142
  67.2 8.9 %copy-start.29 = (s32[1024]{0:T(1024)}, s32[1024]{0:T(1024)S(1)}, u32[]{:S(2)}) copy-start(s32[1024]{0:T(1024)S(1)} %pad_clamp_fusion) | copy-start | bytes 12292
  76.4 1.0 copy-start.5
  85.7 35.6 %copy-start.18 = (bf16[128,1024]{1,0:T(8,128)(2,1)S(1)}, bf16[128,1024]{1,0:T(8,128)(2,1)}, u32[]{:S(2)}) copy-start(bf16[128,1024]{1,0:T(8,128)(2,1)} %param.30) | copy-start | bytes 786436
  125.0 1.2 copy-start.7
  125.0 1.2 copy-start.19
  125.0 2.8 %copy-start.30 = (pred[2,16]{1,0:T(4,128)(4,1)S(1)}, pred[2,16]{1,0:T(4,128)(4,1)}, u32[]{:S(2)}) copy-start(pred[2,16]{1,0:T(4,128)(4,1)} %iota_compare_fusion.2) | copy-start | bytes 100
  125.0 2.9 %copy-start.12 = (f32[2,16,16,64]{3,2,1,0:T(8,128)S(1)}, f32[2,16,16,64]{3,2,1,0:T(8,128)}, u32[]{:S(2)}) copy-start(f32[2,16,16,64]{3,2,1,0:T(8,128)} %reshape.403) | copy-start | bytes 393220
  125.0 2.9 %copy-start.13 = (f32[2,16,16,64]{3,2,1,0:T(8,128)S(1)}, f32[2,16,16,64]{3,2,1,0:T(8,128)}, u32[]{:S(2)}) copy-start(f32[2,16,16,64]{3,2,1,0:T(8,128)} %reshape.404) | copy-start | bytes 393220
  126.3 2.9 %slice-start = ((f32[416,1024]{1,0:T(8,128)}), f32[384,1024]{1,0:T(8,128)S(1)}, s32[]{:S(2)}) async-start(f32[416,1024]{1,0:T(8,128)} %copy-done.7), calls=%async_computation.6 | async-start | bytes 3145728 | tf_op jit(solution)/shard_map/slice | solution.py:180
  139.7 2.1 copy-start.3
  149.7 2.1 copy-start.3
  159.8 2.1 copy-start.3
  169.8 2.1 copy-start.3
  179.9 2.1 copy-start.3
  189.9 2.1 copy-start.3
  197.9 3.7 %copy-start.6 = (f32[2,64,16,64]{3,2,1,0:T(8,128)S(1)}, f32[2,64,16,64]{3,2,1,0:T(8,128)}, u32[]{:S(2)}) copy-start(f32[2,64,16,64]{3,2,1,0:T(8,128)} %copy-done.5) | copy-start | bytes 1572868
  201.2 1.0 copy-start.11
  204.2 12.2 %copy-start.14 = (f32[2,16,16,64]{3,2,1,0:T(8,128)S(1)}, f32[2,16,16,64]{3,2,1,0:T(8,128)}, u32[]{:S(2)}) copy-start(f32[2,16,16,64]{3,2,1,0:T(8,128)} %get-tuple-element.190) | copy-start | bytes 393220
  205.5 12.2 %copy-start.9 = (f32[2,16,16,64]{3,2,1,0:T(8,128)S(1)}, f32[2,16,16,64]{3,2,1,0:T(8,128)}, u32[]{:S(2)}) copy-start(f32[2,16,16,64]{3,2,1,0:T(8,128)} %get-tuple-element.189) | copy-start | bytes 393220
  205.5 12.2 %copy-start.10 = (f32[2,16,16,64]{3,2,1,0:T(8,128)S(1)}, f32[2,16,16,64]{3,2,1,0:T(8,128)}, u32[]{:S(2)}) copy-start(f32[2,16,16,64]{3,2,1,0:T(8,128)} %get-tuple-element.191) | copy-start | bytes 393220
  205.5 12.2 %copy-start.28 = (pred[16,16]{1,0:T(8,128)(4,1)S(1)}, pred[16,16]{1,0:T(8,128)(4,1)}, u32[]{:S(2)}) copy-start(pred[16,16]{1,0:T(8,128)(4,1)} %iota_compare_fusion.1) | copy-start | bytes 772
  205.5 29.9 %all-to-all-start.2 = ((f32[2,64,1024]{2,0,1:T(2,128)}), f32[2,64,1024]{2,0,1:T(2,128)S(1)}, u32[]{:S(2)}, u32[]{:S(2)}) async-start(f32[2,64,1024]{2,0,1:T(2,128)} %reshape.497), calls=%async_computation.2 | async-start | bytes 1048576 | tf_op jit(solution)/shard_map/all_to_all | solution.py:222
  216.4 2.5 %copy-start.4 = (f32[6,64,16,64]{3,1,2,0:T(8,128)S(1)}, f32[6,64,16,64]{3,1,2,0:T(8,128)}, u32[]{:S(2)}) copy-start(f32[6,64,16,64]{3,1,2,0:T(8,128)} %get-tuple-element.79) | copy-start | bytes 4718596
  229.2 1.6 copy-start.26
  229.2 1.6 copy-start.27
  235.8 2.4 copy-start.1
Sparse Core Ops, SparseCore 0:
  36.2 38.7 all-gather.4
  76.7 44.5 all-gather.2
where the time goes:
time: 246 us; the launch traced here: 245 us
  waiting for transfers between devices  54.8 us (22%)
  local copies, waits for them, and re-layouts  52.2 us (21%)
  matrix products  46.3 us (19%)
  other arithmetic  43.6 us (18%)
  starting transfers between devices  33.1 us (13%)
  between operations  14.8 us (6%)
    all_gather x1, waiting for transfers between devices, project(): lax.all_gather(decay_mixed_input, 'tp', axis=1, tiled=True)  33.6 us
    mul x6, other arithmetic, one_block(): keys_scaled = address_vectors_all * jnp.exp(middle - inclusive)  15 us
    all_to_all x1, starting transfers between devices, local(): lax.all_to_all(ordered_shift, 'rep', split_axis=0, concat_axis=1, tiled=T...  13 us
    dot_general x7, matrix products, one_block(): jnp.einsum('thi,hij->thj', accept_vectors_all * jnp.exp(exclusive), threa...  11.9 us
    all_to_all x1, starting transfers between devices, local(): lax.all_to_all(ret_state, 'rep', split_axis=1, concat_axis=0, tiled=True)  10.8 us
    dot_general x7, matrix products, one_block(): jnp.einsum('thi,shi->hts', recept_scaled, keys_scaled, precision=HIGH)  8.27 us
    dot_general x1, matrix products, project(): jnp.dot(lax.all_gather(mixed_value, 'tp', axis=1, tiled=True), content_ma...  8.09 us
    another operation x7, other arithmetic, one_block(): inclusive = jnp.cumsum(rate_b, axis=0)  8.08 us
  transfers between devices with their start and end apart: 6, of which 4 were waited for; matrix products, arithmetic and copies ran while one was open for 20% of the time, Pallas kernels for 0%

commit v1 on v0

--- a/solution.py
+++ b/solution.py
@@ -35,7 +35,9 @@
         preferred_element_type=jnp.float32,
     )
     decay_accumulated = jnp.dot(
-        lax.all_gather(decay_mixed_input, "tp", axis=1, tiled=True),
+        jnp.concatenate(
+            lax.all_to_all(jnp.stack([decay_mixed_input] * lax.axis_size("tp")), "tp", 0, 0), axis=1
+        ),
         forget_shrink_map,
         preferred_element_type=jnp.float32,
     )

time: 246 us -> 284 us (1.15)
  waiting for transfers between devices: 54.8 us -> 72 us
  starting transfers between devices: 33.1 us -> 43.9 us
  local copies, waits for them, and re-layouts: 52.2 us -> 62.1 us
    all_to_all x0 -> x1, waiting for transfers between devices: none -> 47.4 us  [project(): lax.all_to_all(jnp.stack([decay_mixed_input] * lax.axis_size('tp')), 'tp'...]
    all_gather x1 -> x0, waiting for transfers between devices: 33.6 us -> none  [project(): lax.all_gather(decay_mixed_input, 'tp', axis=1, tiled=True)]
    all_to_all x1, waiting for transfers between devices: 6.69 us -> 16.6 us  [local(): lax.all_to_all(ordered_state, 'rep', split_axis=0, concat_axis=1, tiled=T...]
    all_to_all x1, waiting for transfers between devices: 7.31 us -> 0.56 us  [local(): lax.all_to_all(ordered_shift, 'rep', split_axis=0, concat_axis=1, tiled=T...]
    all_to_all x1, starting transfers between devices: 4.42 us -> 9.74 us  [local(): lax.all_to_all(ret_shift, 'rep', split_axis=1, concat_axis=0, tiled=True)]
    all_to_all x0 -> x1, starting transfers between devices: none -> 4.84 us  [project(): lax.all_to_all(jnp.stack([decay_mixed_input] * lax.axis_size('tp')), 'tp'...]
    reshape x0 -> x1, local copies, waits for them, and re-layouts: none -> 4.29 us  [project(): jnp.concatenate(lax.all_to_all(jnp.stack([decay_mixed_input] * lax.axis_s...]
    unnamed x66 -> x60, local copies, waits for them, and re-layouts: 5.77 us -> 6.57 us
  transfers between devices with their start and end apart: 6 -> 6, of which waited for: 4 -> 4; matrix products, arithmetic and copies ran while one was open for 20% -> 22% of each run, Pallas kernels for 0% -> 0%
where the time goes in v1:
time: 284 us; the launch traced here: 283 us
  waiting for transfers between devices  72 us (25%)
  local copies, waits for them, and re-layouts  62.1 us (22%)
  matrix products  47.1 us (17%)
  starting transfers between devices  43.9 us (15%)
  other arithmetic  42.8 us (15%)
  between operations  14.7 us (5%)
    all_to_all x1, waiting for transfers between devices, project(): lax.all_to_all(jnp.stack([decay_mixed_input] * lax.axis_size('tp')), 'tp'...  47.4 us
    all_to_all x1, waiting for transfers between devices, local(): lax.all_to_all(ordered_state, 'rep', split_axis=0, concat_axis=1, tiled=T...  16.6 us
    mul x6, other arithmetic, one_block(): keys_scaled = address_vectors_all * jnp.exp(middle - inclusive)  15 us
    all_to_all x1, starting transfers between devices, local(): lax.all_to_all(ordered_shift, 'rep', split_axis=0, concat_axis=1, tiled=T...  13 us
    dot_general x7, matrix products, one_block(): jnp.einsum('thi,hij->thj', accept_vectors_all * jnp.exp(exclusive), threa...  11.9 us
    all_to_all x1, starting transfers between devices, local(): lax.all_to_all(ret_state, 'rep', split_axis=1, concat_axis=0, tiled=True)  10.8 us
    all_to_all x1, starting transfers between devices, local(): lax.all_to_all(ret_shift, 'rep', split_axis=1, concat_axis=0, tiled=True)  9.74 us
    dot_general x7, matrix products, one_block(): jnp.einsum('thi,shi->hts', recept_scaled, keys_scaled, precision=HIGH)  8.99 us
  transfers between devices with their start and end apart: 6, of which 4 were waited for; matrix products, arithmetic and copies ran while one was open for 22% of the time, Pallas kernels for 0%

profile of v1, /device:TPU:1, one launch (start us, length us, event | category | flops | bytes accessed | tf_op | source)
XLA Modules:
  0.0 282.9 jit_solution(13091516846290941439)
XLA Ops:
  10.2 13.0 %all-to-all-start.1 = ((bf16[128,1,16]{2,1,0:T(2,128)(2,1)}), bf16[128,1,16]{2,1,0:T(2,128)(2,1)S(1)}, u32[]{:S(2)}, u32[]{:S(2)}) async-start(bf16[128,1,16]{2,1,0:T(2,128)(2,1)} %convert.36), calls=%async_computation.1 | async-start | bytes 131072 | tf_op jit(solution)/shard_map/all_to_all | solution.py:145
  23.2 1.3 gather_fusion
  24.5 1.3 gather_fusion.4
  27.6 1.1 copy.242
  28.8 1.6 gather_fusion.2
  30.4 2.4 copy.157
  34.4 9.7 %all-to-all-start.4 = ((bf16[2,64,16]{2,0,1:T(2,128)(2,1)}), bf16[2,64,16]{2,0,1:T(2,128)(2,1)S(1)}, u32[]{:S(2)}, u32[]{:S(2)}) async-start(bf16[2,64,16]{2,0,1:T(2,128)(2,1)} %convert_bitcast_fusion), calls=%async_computation.4 | async-start | bytes 65536 | tf_op jit(solution)/shard_map/all_to_all | solution.py:225
  44.1 1.7 fusion.18
  45.9 7.5 %all-to-all-done.4 = bf16[2,64,16]{2,0,1:T(2,128)(2,1)S(1)} async-done(((bf16[2,64,16]{2,0,1:T(2,128)(2,1)}), bf16[2,64,16]{2,0,1:T(2,128)(2,1)S(1)}, u32[]{:S(2)}, u32[]{:S(2)}) %all-to-all-start.4) | async-done | bytes 4128 | tf_op jit(solution)/shard_map/all_to_all | solution.py:225
  53.4 5.5 %all-to-all-start = ((f32[128,1,1024]{2,1,0:T(1,128)}), f32[128,1,1024]{2,1,0:T(1,128)}, u32[]{:S(2)}, u32[]{:S(2)}) async-start(f32[128,1,1024]{2,1,0:T(1,128)} %copy.157), calls=%async_computation | async-start | bytes 1048576 | tf_op jit(solution)/shard_map/all_to_all | solution.py:144
  60.1 16.6 %all-to-all-done = f32[128,1,1024]{2,1,0:T(1,128)} async-done(((f32[128,1,1024]{2,1,0:T(1,128)}), f32[128,1,1024]{2,1,0:T(1,128)}, u32[]{:S(2)}, u32[]{:S(2)}) %all-to-all-start) | async-done | bytes 524320 | tf_op jit(solution)/shard_map/all_to_all | solution.py:144
  76.7 2.2 stack.2
  78.9 4.8 %all-to-all-start.2 = ((bf16[4,416,1024]{2,1,0:T(8,128)(2,1)}), bf16[4,416,1024]{2,1,0:T(8,128)(2,1)}, u32[]{:S(2)}, u32[]{:S(2)}) async-start(bf16[4,416,1024]{2,1,0:T(8,128)(2,1)} %stack.2), calls=%async_computation.2 | async-start | bytes 6815744 | tf_op jit(solution)/shard_map/all_to_all | solution.py:39
  83.8 1.2 scatter_custom_fusion
  86.7 2.1 reshape.412
  88.8 2.2 reshape.410
  93.6 1.2 copy.243
  96.3 47.4 %all-to-all-done.2 = bf16[4,416,1024]{2,1,0:T(8,128)(2,1)} async-done(((bf16[4,416,1024]{2,1,0:T(8,128)(2,1)}), bf16[4,416,1024]{2,1,0:T(8,128)(2,1)}, u32[]{:S(2)}, u32[]{:S(2)}) %all-to-all-start.2) | async-done | bytes 3407904 | tf_op jit(solution)/shard_map/all_to_all | solution.py:39
  143.7 4.3 %copy.205 = bf16[4,52,8,1024]{3,2,0,1:T(8,128)(2,1)} copy(bf16[4,52,8,1024]{3,2,1,0:T(8,128)(2,1)} %bitcast.58) | data formatting | bytes 6815744 | tf_op jit(solution)/shard_map/reshape | solution.py:38
  147.9 3.7 %exponential_negate_fusion = f32[416,1024]{1,0:T(8,128)S(1)} fusion(bf16[128,1024]{1,0:T(8,128)(2,1)S(1)} %copy-done.15, bf16[416,4096]{1,0:T(8,128)(2,1)} %bitcast.184, bf16[4096,128]{1,0:T(8,128)(2,1)S(1)} %copy-done, f32[1024]{0:T(1024)} %param.31), kind=kOutput, calls=%fused_computation.44 | convolution fusion | flops 546164736 | bytes 6426624 | tf_op jit(solution)/shard_map/dot_general | solution.py:49
  151.7 1.1 copy-done.6
  153.1 1.4 fusion.41
  154.5 1.9 select_multiply_fusion
  157.1 2.1 reshape_reshape.7
  159.8 1.4 convolution_select_fusion.1
  161.2 8.1 %convolution_convert_fusion = bf16[416,1024]{1,0:T(8,128)(2,1)S(1)} fusion(bf16[416,4096]{1,0:T(8,128)(2,1)} %all-gather.2.cloned.1.call-done, bf16[4096,1024]{1,0:T(8,128)(2,1)} %param.28), kind=kOutput, calls=%fused_computation.48 | convolution fusion | flops 3490086912 | bytes 12648448 | tf_op jit(solution)/shard_map/dot_general | solution.py:32
  169.6 2.1 reshape.411
  171.7 60.3 %while.3 = (s32[]{:T(128)}, f32[16,64,64]{2,1,0:T(8,128)S(1)}, f32[6,64,16,64]{3,1,2,0:T(8,128)}, f32[6,64,16,64]{3,2,1,0:T(8,128)}, f32[6,64,16,64]{3,2,1,0:T(8...) while((s32[]{:T(128)}, f32[16,64,64]{2,1,0:T(8,128)S(1)}, ...), condition=%wide.region_3.4_spmd.clone, body=%wide.region_0.3_spmd.clone.sunk | while | flops 206572544 | bytes 8724625 | solution.py:94
  174.0 2.5 bitcast_multiply_fusion.6
  176.6 1.3 convolution_select_fusion.3
  178.7 1.8 fusion.70
  180.4 1.3 convolution_add_fusion.3
  184.1 2.5 bitcast_multiply_fusion.6
  186.6 1.3 convolution_select_fusion.3
  188.7 1.8 fusion.70
  190.5 1.3 convolution_add_fusion.3
  194.1 2.5 bitcast_multiply_fusion.6
  196.7 1.3 convolution_select_fusion.3
  198.8 1.8 fusion.70
  200.6 1.3 convolution_add_fusion.3
  204.2 2.5 bitcast_multiply_fusion.6
  206.8 1.3 convolution_select_fusion.3
  208.8 1.8 fusion.70
  210.6 1.3 convolution_add_fusion.3
  214.2 2.5 bitcast_multiply_fusion.6
  216.8 1.3 convolution_select_fusion.3
  218.9 1.8 fusion.70
  220.6 1.3 convolution_add_fusion.3
  224.3 2.5 bitcast_multiply_fusion.6
  226.8 1.3 convolution_select_fusion.3
  228.9 1.8 fusion.70
  230.7 1.3 convolution_add_fusion.3
  232.0 2.8 reduce_sum.64
  234.8 3.3 %multiply_reduce_fusion = f32[6,64,16]{1,2,0:T(8,128)S(1)} fusion(f32[6,64,16,64]{3,1,2,0:T(8,128)} %get-tuple-element.79, f32[6,64,16]{1,2,0:T(8,128)S(1)} %broadcast_multiply_fusion), kind=kLoop, calls=%fused_computation.40 | loop fusion | flops 1173504 | bytes 1622016 | tf_op jit(solution)/shard_map/reduce_sum | solution.py:14
  238.9 1.4 fusion.19
  240.9 1.3 reshape.507
  242.2 10.8 %all-to-all-start.3 = ((f32[2,64,1024]{2,0,1:T(2,128)}), f32[2,64,1024]{2,0,1:T(2,128)S(1)}, u32[]{:S(2)}, u32[]{:S(2)}) async-start(f32[2,64,1024]{2,0,1:T(2,128)} %reshape.507), calls=%async_computation.3 | async-start | bytes 1048576 | tf_op jit(solution)/shard_map/all_to_all | solution.py:224
  253.1 1.3 fusion.24
  254.8 5.3 %copy.167 = f32[6,64,16,64]{3,2,1,0:T(8,128)} copy(f32[6,64,16,64]{3,1,2,0:T(8,128)} %get-tuple-element.79) | data formatting | bytes 3145728 | tf_op jit(solution)/shard_map/while | solution.py:94
  260.2 3.7 %reshape.407 = f32[1,384,1024]{2,1,0:T(8,128)} reshape(f32[6,64,16,64]{3,2,1,0:T(8,128)} %copy.167) | data formatting | bytes 3145728 | tf_op jit(solution)/shard_map/reshape | solution.py:105
  265.3 1.6 copy.169
  267.1 1.6 copy.171
  269.4 3.9 %fusion.26 = bf16[1,384,1024]{2,1,0:T(8,128)(2,1)} fusion(f32[1024]{0:T(1024)S(1)} %copy-done.23, f32[1024]{0:T(1024)S(1)} %copy-done.24, f32[1,384,1024]{2,1,0:T(8,128)} %copy.171, f32[1,384,1024]{2,1,0:T(8,128)} %reshape.407, f32[1,384,1024]{2,1,0:T(8,128)} %copy.169, pred[]{:T(512)S(1)} %bitcast.204), kind=kLoop, calls=%fused_computation.66 | loop fusion | flops 2359296 | bytes 5513217 | tf_op jit(solution)/shard_map/jit(_where)/select_n | solution.py:187
  274.7 1.3 copy.192
  (201 shorter events, 39.5 us)
Async XLA Ops:
  7.2 140.8 %copy-start = (bf16[4096,128]{1,0:T(8,128)(2,1)S(1)}, bf16[4096,128]{1,0:T(8,128)(2,1)}, u32[]{:S(2)}) copy-start(bf16[4096,128]{1,0:T(8,128)(2,1)} %param.29) | copy-start | bytes 3145732
  7.2 18.7 %copy-start.2 = (s32[128]{0:T(128)S(1)}, s32[128]{0:T(128)}, u32[]{:S(2)}) copy-start(s32[128]{0:T(128)} %param.40) | copy-start | bytes 1540
  7.2 19.3 %copy-start.7 = (bf16[1,384,1024]{2,1,0:T(8,128)(2,1)S(1)}, bf16[1,384,1024]{2,1,0:T(8,128)(2,1)}, u32[]{:S(2)}) copy-start(bf16[1,384,1024]{2,1,0:T(8,128)(2,1)} %param.22) | copy-start | bytes 2359300
  9.5 17.1 %copy-start.14 = (bf16[2,16,1024]{2,1,0:T(8,128)(2,1)S(1)}, bf16[2,16,1024]{2,1,0:T(8,128)(2,1)}, u32[]{:S(2)}) copy-start(bf16[2,16,1024]{2,1,0:T(8,128)(2,1)} %param.25) | copy-start | bytes 196612
  10.2 23.1 %all-to-all-start.1 = ((bf16[128,1,16]{2,1,0:T(2,128)(2,1)}), bf16[128,1,16]{2,1,0:T(2,128)(2,1)S(1)}, u32[]{:S(2)}, u32[]{:S(2)}) async-start(bf16[128,1,16]{2,1,0:T(2,128)(2,1)} %convert.36), calls=%async_computation.1 | async-start | bytes 131072 | tf_op jit(solution)/shard_map/all_to_all | solution.py:145
  28.8 15.4 %copy-start.21 = (f32[1024]{0:T(1024)S(1)}, f32[1024]{0:T(1024)}, u32[]{:S(2)}) copy-start(f32[1024]{0:T(1024)} %param.33) | copy-start | bytes 12292
  28.8 15.4 %copy-start.22 = (f32[1024]{0:T(1024)S(1)}, f32[1024]{0:T(1024)}, u32[]{:S(2)}) copy-start(f32[1024]{0:T(1024)} %param.34) | copy-start | bytes 12292
  34.4 19.0 %all-to-all-start.4 = ((bf16[2,64,16]{2,0,1:T(2,128)(2,1)}), bf16[2,64,16]{2,0,1:T(2,128)(2,1)S(1)}, u32[]{:S(2)}, u32[]{:S(2)}) async-start(bf16[2,64,16]{2,0,1:T(2,128)(2,1)} %convert_bitcast_fusion), calls=%async_computation.4 | async-start | bytes 65536 | tf_op jit(solution)/shard_map/all_to_all | solution.py:225
  45.8 13.2 %copy-start.9 = (bf16[384,1024]{1,0:T(8,128)(2,1)S(1)}, bf16[384,1024]{1,0:T(8,128)(2,1)}, u32[]{:S(2)}) copy-start(bf16[384,1024]{1,0:T(8,128)(2,1)} %get-tuple-element.184) | copy-start | bytes 2359300
  45.9 14.2 %copy-start.8 = (bf16[384,1024]{1,0:T(8,128)(2,1)S(1)}, bf16[384,1024]{1,0:T(8,128)(2,1)}, u32[]{:S(2)}) copy-start(bf16[384,1024]{1,0:T(8,128)(2,1)} %get-tuple-element.185) | copy-start | bytes 2359300
  53.4 23.3 %all-to-all-start = ((f32[128,1,1024]{2,1,0:T(1,128)}), f32[128,1,1024]{2,1,0:T(1,128)}, u32[]{:S(2)}, u32[]{:S(2)}) async-start(f32[128,1,1024]{2,1,0:T(1,128)} %copy.157), calls=%async_computation | async-start | bytes 1048576 | tf_op jit(solution)/shard_map/all_to_all | solution.py:144
  59.0 102.2 %all-gather.2.cloned.1.call-start = ((), (), s32[]{:S(2)}) async-start(), calls=%async_computation.5 | async-start | bytes 4259840 | tf_op jit(solution)/shard_map/all_gather | solution.py:33
  78.9 6.0 %copy-start.16 = (f32[1024]{0:T(1024)S(1)}, f32[1024]{0:T(1024)}, u32[]{:S(2)}) copy-start(f32[1024]{0:T(1024)} %param.32) | copy-start | bytes 12292
  78.9 6.1 %copy-start.18 = (bf16[2,16,1024]{2,1,0:T(8,128)(2,1)S(1)}, bf16[2,16,1024]{2,1,0:T(8,128)(2,1)}, u32[]{:S(2)}) copy-start(bf16[2,16,1024]{2,1,0:T(8,128)(2,1)} %param.26) | copy-start | bytes 196612
  78.9 7.0 %copy-start.19 = (bf16[2,16,1024]{2,1,0:T(8,128)(2,1)S(1)}, bf16[2,16,1024]{2,1,0:T(8,128)(2,1)}, u32[]{:S(2)}) copy-start(bf16[2,16,1024]{2,1,0:T(8,128)(2,1)} %param.27) | copy-start | bytes 196612
  78.9 7.8 %copy-start.12 = (bf16[1,384,1024]{2,1,0:T(8,128)(2,1)S(1)}, bf16[1,384,1024]{2,1,0:T(8,128)(2,1)}, u32[]{:S(2)}) copy-start(bf16[1,384,1024]{2,1,0:T(8,128)(2,1)} %param.23) | copy-start | bytes 2359300
  78.9 64.7 %all-to-all-start.2 = ((bf16[4,416,1024]{2,1,0:T(8,128)(2,1)}), bf16[4,416,1024]{2,1,0:T(8,128)(2,1)}, u32[]{:S(2)}, u32[]{:S(2)}) async-start(bf16[4,416,1024]{2,1,0:T(8,128)(2,1)} %stack.2), calls=%async_computation.2 | async-start | bytes 6815744 | tf_op jit(solution)/shard_map/all_to_all | solution.py:39
  86.7 2.1 copy-start.13
  91.6 4.5 %copy-start.26 = (s32[1024]{0:T(1024)}, s32[1024]{0:T(1024)S(1)}, u32[]{:S(2)}) copy-start(s32[1024]{0:T(1024)S(1)} %pad_clamp_fusion) | copy-start | bytes 12292
  95.1 1.0 copy-start.4
  143.7 4.3 %copy-start.15 = (bf16[128,1024]{1,0:T(8,128)(2,1)S(1)}, bf16[128,1024]{1,0:T(8,128)(2,1)}, u32[]{:S(2)}) copy-start(bf16[128,1024]{1,0:T(8,128)(2,1)} %param.30) | copy-start | bytes 786436
  151.6 1.2 copy-start.6
  151.7 1.3 copy-start.27
  152.9 4.1 %slice-start = ((f32[416,1024]{1,0:T(8,128)}), f32[384,1024]{1,0:T(8,128)S(1)}, s32[]{:S(2)}) async-start(f32[416,1024]{1,0:T(8,128)} %copy-done.6), calls=%async_computation.6 | async-start | bytes 3145728 | tf_op jit(solution)/shard_map/slice | solution.py:182
  157.1 2.7 copy-start.25
  176.6 2.1 copy-start.3
  186.6 2.1 copy-start.3
  196.7 2.1 copy-start.3
  206.8 2.1 copy-start.3
  216.8 2.1 copy-start.3
  226.8 2.1 copy-start.3
  234.8 3.7 %copy-start.5 = (f32[2,64,16,64]{3,2,1,0:T(8,128)S(1)}, f32[2,64,16,64]{3,2,1,0:T(8,128)}, u32[]{:S(2)}) copy-start(f32[2,64,16,64]{3,2,1,0:T(8,128)} %copy-done.4) | copy-start | bytes 1572868
  238.2 0.7 copy-start.17
  240.9 12.2 %copy-start.10 = (f32[2,16,16,64]{3,2,1,0:T(8,128)S(1)}, f32[2,16,16,64]{3,2,1,0:T(8,128)}, u32[]{:S(2)}) copy-start(f32[2,16,16,64]{3,2,1,0:T(8,128)} %get-tuple-element.190) | copy-start | bytes 393220
  242.2 12.2 %copy-start.11 = (f32[2,16,16,16]{3,2,1,0:T(8,128)S(1)}, f32[2,16,16,16]{3,2,1,0:T(8,128)}, u32[]{:S(2)}) copy-start(f32[2,16,16,16]{3,2,1,0:T(8,128)} %convolution_select_fusion.1) | copy-start | bytes 98308
  242.2 12.2 %copy-start.20 = (f32[2,16,16]{1,2,0:T(8,128)S(1)}, f32[2,16,16]{1,2,0:T(8,128)}, u32[]{:S(2)}) copy-start(f32[2,16,16]{1,2,0:T(8,128)} %copy.178) | copy-start | bytes 6148
  242.2 31.0 %all-to-all-start.3 = ((f32[2,64,1024]{2,0,1:T(2,128)}), f32[2,64,1024]{2,0,1:T(2,128)S(1)}, u32[]{:S(2)}, u32[]{:S(2)}) async-start(f32[2,64,1024]{2,0,1:T(2,128)} %reshape.507), calls=%async_computation.3 | async-start | bytes 1048576 | tf_op jit(solution)/shard_map/all_to_all | solution.py:224
  267.0 1.7 copy-start.23
  267.0 1.7 copy-start.24
  273.6 2.4 copy-start.1
Sparse Core Ops, SparseCore 0:
  61.6 63.9 all-gather.1
